TPU v7x, 256 devices: a whole 4x4x8 slice. The times are simulated.
256 devices in a mesh: blk: 16 (over x, z_lo, core), grp: 16 (over z_hi, y).
Axes of the slice: x: 4, y: 4, z: 8 (z_hi: 4, z_lo: 2; z = z_hi * 2 + z_lo), core: 2. Of those that a mesh axis runs over, the one named last changes fastest.
Arguments:
- amplitudes: bfloat16 [12288, 1024], P(('blk', 'grp')), may hold values from -6 to 6
- integrals: bfloat16 [1024, 65536], P(None, ('grp', 'blk')), may hold values from -0.1875 to 0.1875
- amplitude_mask: int32 [768, 8], P(('blk', 'grp')), may hold values 0 or 1
- integral_mask: int32 [8, 512], P(None, ('grp', 'blk')), may hold values 0 or 1
Outputs:
- residual: bfloat16 [12288, 65536], P('blk', 'grp')
All inputs are finite; a program needn't handle non-finite values. No bound on the sum of `amplitude_mask` or of `integral_mask` on one device may be relied on, other than what follows from the above.
Results may differ from a plain program's by a relative error of at most 0.001.
Values may be sent and summed in bfloat16 or wider, within the bound.
A program may use at most 64 MiB of HBM per device.

v0:
```python
import jax
import jax.numpy as jnp
from jax import lax
from jax.sharding import PartitionSpec as P

TILE = 128
OTILE = 16


def shifted(block, axis, distance):
    devices = range(lax.axis_size(axis))
    route = [((i - distance) % len(devices), i) for i in devices]
    return lax.ppermute(block, axis, route)


def mask_tiles(values, screen, row_tile, col_tile):
    height, breadth = values.shape
    tiled = values.reshape(height // row_tile, row_tile, breadth // col_tile, col_tile)
    tiled = tiled * screen.astype(values.dtype)[:, None, :, None]
    return tiled.reshape(height, breadth)


def local(amplitudes, integrals, amplitude_mask, integral_mask):
    amp_masked = mask_tiles(amplitudes, amplitude_mask, OTILE, TILE)
    int_panel = mask_tiles(integrals, integral_mask, TILE, TILE)
    gathered = lax.all_gather(amp_masked, "grp", axis=0, tiled=True)

    def contract(segment):
        return (0.5 * jnp.dot(gathered, segment, preferred_element_type=jnp.float32)).astype(
            jnp.bfloat16
        )

    cycle_size = lax.axis_size("blk")
    panel_width = int_panel.shape[1]
    position = lax.axis_index("blk")
    result = jnp.zeros((gathered.shape[0], cycle_size * panel_width), jnp.bfloat16)
    result = lax.dynamic_update_slice_in_dim(result, contract(int_panel), position * panel_width, 1)

    def advance(turn_index, carry):
        current, result = carry
        current = shifted(current, "blk", 1)
        owner = (position - turn_index) % cycle_size
        result = lax.dynamic_update_slice_in_dim(result, contract(current), owner * panel_width, 1)
        return (current, result)

    current, result = lax.fori_loop(1, cycle_size, advance, (int_panel, result))
    return result


def solution(mesh):
    return jax.shard_map(
        local,
        mesh=mesh,
        in_specs=(
            P(("blk", "grp"), None),
            P(None, ("grp", "blk")),
            P(("blk", "grp"), None),
            P(None, ("grp", "blk")),
        ),
        out_specs=P("blk", "grp"),
        check_vma=False,
    )
```

profile of v0, /device:TPU:8, one launch (start us, length us, event | category | flops | bytes accessed | tf_op | source)
XLA Modules:
  0.0 262.3 jit_solution(9153554101730459474)
XLA Ops:
  6.5 0.7 convert_element_type.20
  7.2 0.1 mul.51
  7.3 1.6 bitcast_multiply_fusion.1
  8.9 0.0 all-gather.2.cloned.1.call-update
  8.9 0.7 convert_element_type.19
  9.6 0.1 copy.5
  9.7 0.3 mul.48
  10.0 1.1 bitcast_multiply_fusion
  11.1 58.3 %all-gather.2.cloned.1.call-done = bf16[768,1024]{1,0:T(8,128)(2,1)} async-done(((bf16[48,1024]{1,0:T(8,128)(2,1)}), bf16[768,1024]{1,0:T(8,128)(2,1)}) %all-gather.2.cloned.1.call-update) | async-done | bytes 1572880 | tf_op jit(solution)/shard_map/all_gather | solution.py:26
  69.5 0.8 broadcast_in_dim.2
  70.3 0.6 copy-done.1
  70.9 0.6 fusion.3
  71.5 0.0 copy-start
  71.5 2.7 %copy-done = bf16[768,4096]{1,0:T(8,128)(2,1)} copy-done((bf16[768,4096]{1,0:T(8,128)(2,1)}, bf16[768,4096]{1,0:T(8,128)(2,1)S(1)}, u32[]{:S(2)}) %copy-start) | copy-done | bytes 6291480
  74.2 181.3 %while.17 = (s32[]{:T(128)}, bf16[1024,256]{1,0:T(8,128)(2,1)S(1)}, bf16[768,4096]{1,0:T(8,128)(2,1)}, bf16[768,1024]{1,0:T(8,128)(2,1)S(1)}, s32[]{:T(128)}, /*...) while((s32[]{:T(128)}, bf16[1024,256]{1,0:T(8,128)(2,1)S(1)}, ...), condition=%wide.region_1.2_spmd, body=%wide.region_0.1_spmd.sunk | while | flops 403046432 | bytes 5636416 | solution.py:46
  74.2 0.0 collective-permute-start
  74.2 10.7 %collective-permute-done = bf16[1024,256]{1,0:T(8,128)(2,1)S(1)} collective-permute-done((bf16[1024,256]{1,0:T(8,128)(2,1)S(1)}, bf16[1024,256]{1,0:T(8,128)(2,1)S(1)}, u32[]{:S(2)}, u32[]{:S(2)}) %collective-permute-start) | collective-permute-done | bytes 524320 | tf_op jit(solution)/shard_map/while/body/eval_jaxpr/ppermute | solution.py:13
  84.9 1.3 fusion.13
  86.3 10.7 %collective-permute-done = bf16[1024,256]{1,0:T(8,128)(2,1)S(1)} collective-permute-done((bf16[1024,256]{1,0:T(8,128)(2,1)S(1)}, bf16[1024,256]{1,0:T(8,128)(2,1)S(1)}, u32[]{:S(2)}, u32[]{:S(2)}) %collective-permute-start) | collective-permute-done | bytes 524320 | tf_op jit(solution)/shard_map/while/body/eval_jaxpr/ppermute | solution.py:13
  97.0 1.3 fusion.13
  98.3 10.7 %collective-permute-done = bf16[1024,256]{1,0:T(8,128)(2,1)S(1)} collective-permute-done((bf16[1024,256]{1,0:T(8,128)(2,1)S(1)}, bf16[1024,256]{1,0:T(8,128)(2,1)S(1)}, u32[]{:S(2)}, u32[]{:S(2)}) %collective-permute-start) | collective-permute-done | bytes 524320 | tf_op jit(solution)/shard_map/while/body/eval_jaxpr/ppermute | solution.py:13
  109.1 1.3 fusion.13
  110.4 0.0 collective-permute-start
  110.4 10.7 %collective-permute-done = bf16[1024,256]{1,0:T(8,128)(2,1)S(1)} collective-permute-done((bf16[1024,256]{1,0:T(8,128)(2,1)S(1)}, bf16[1024,256]{1,0:T(8,128)(2,1)S(1)}, u32[]{:S(2)}, u32[]{:S(2)}) %collective-permute-start) | collective-permute-done | bytes 524320 | tf_op jit(solution)/shard_map/while/body/eval_jaxpr/ppermute | solution.py:13
  121.2 1.3 fusion.13
  122.5 0.0 collective-permute-start
  122.5 10.7 %collective-permute-done = bf16[1024,256]{1,0:T(8,128)(2,1)S(1)} collective-permute-done((bf16[1024,256]{1,0:T(8,128)(2,1)S(1)}, bf16[1024,256]{1,0:T(8,128)(2,1)S(1)}, u32[]{:S(2)}, u32[]{:S(2)}) %collective-permute-start) | collective-permute-done | bytes 524320 | tf_op jit(solution)/shard_map/while/body/eval_jaxpr/ppermute | solution.py:13
  133.3 1.3 fusion.13
  134.6 10.7 %collective-permute-done = bf16[1024,256]{1,0:T(8,128)(2,1)S(1)} collective-permute-done((bf16[1024,256]{1,0:T(8,128)(2,1)S(1)}, bf16[1024,256]{1,0:T(8,128)(2,1)S(1)}, u32[]{:S(2)}, u32[]{:S(2)}) %collective-permute-start) | collective-permute-done | bytes 524320 | tf_op jit(solution)/shard_map/while/body/eval_jaxpr/ppermute | solution.py:13
  145.3 1.3 fusion.13
  146.7 10.7 %collective-permute-done = bf16[1024,256]{1,0:T(8,128)(2,1)S(1)} collective-permute-done((bf16[1024,256]{1,0:T(8,128)(2,1)S(1)}, bf16[1024,256]{1,0:T(8,128)(2,1)S(1)}, u32[]{:S(2)}, u32[]{:S(2)}) %collective-permute-start) | collective-permute-done | bytes 524320 | tf_op jit(solution)/shard_map/while/body/eval_jaxpr/ppermute | solution.py:13
  157.4 1.3 fusion.13
  158.8 10.7 %collective-permute-done = bf16[1024,256]{1,0:T(8,128)(2,1)S(1)} collective-permute-done((bf16[1024,256]{1,0:T(8,128)(2,1)S(1)}, bf16[1024,256]{1,0:T(8,128)(2,1)S(1)}, u32[]{:S(2)}, u32[]{:S(2)}) %collective-permute-start) | collective-permute-done | bytes 524320 | tf_op jit(solution)/shard_map/while/body/eval_jaxpr/ppermute | solution.py:13
  169.5 1.3 fusion.13
  170.8 10.7 %collective-permute-done = bf16[1024,256]{1,0:T(8,128)(2,1)S(1)} collective-permute-done((bf16[1024,256]{1,0:T(8,128)(2,1)S(1)}, bf16[1024,256]{1,0:T(8,128)(2,1)S(1)}, u32[]{:S(2)}, u32[]{:S(2)}) %collective-permute-start) | collective-permute-done | bytes 524320 | tf_op jit(solution)/shard_map/while/body/eval_jaxpr/ppermute | solution.py:13
  181.6 1.3 fusion.13
  182.9 10.7 %collective-permute-done = bf16[1024,256]{1,0:T(8,128)(2,1)S(1)} collective-permute-done((bf16[1024,256]{1,0:T(8,128)(2,1)S(1)}, bf16[1024,256]{1,0:T(8,128)(2,1)S(1)}, u32[]{:S(2)}, u32[]{:S(2)}) %collective-permute-start) | collective-permute-done | bytes 524320 | tf_op jit(solution)/shard_map/while/body/eval_jaxpr/ppermute | solution.py:13
  193.7 1.3 fusion.13
  195.0 10.7 %collective-permute-done = bf16[1024,256]{1,0:T(8,128)(2,1)S(1)} collective-permute-done((bf16[1024,256]{1,0:T(8,128)(2,1)S(1)}, bf16[1024,256]{1,0:T(8,128)(2,1)S(1)}, u32[]{:S(2)}, u32[]{:S(2)}) %collective-permute-start) | collective-permute-done | bytes 524320 | tf_op jit(solution)/shard_map/while/body/eval_jaxpr/ppermute | solution.py:13
  205.8 1.3 fusion.13
  207.1 10.7 %collective-permute-done = bf16[1024,256]{1,0:T(8,128)(2,1)S(1)} collective-permute-done((bf16[1024,256]{1,0:T(8,128)(2,1)S(1)}, bf16[1024,256]{1,0:T(8,128)(2,1)S(1)}, u32[]{:S(2)}, u32[]{:S(2)}) %collective-permute-start) | collective-permute-done | bytes 524320 | tf_op jit(solution)/shard_map/while/body/eval_jaxpr/ppermute | solution.py:13
  217.8 1.3 fusion.13
  219.2 10.7 %collective-permute-done = bf16[1024,256]{1,0:T(8,128)(2,1)S(1)} collective-permute-done((bf16[1024,256]{1,0:T(8,128)(2,1)S(1)}, bf16[1024,256]{1,0:T(8,128)(2,1)S(1)}, u32[]{:S(2)}, u32[]{:S(2)}) %collective-permute-start) | collective-permute-done | bytes 524320 | tf_op jit(solution)/shard_map/while/body/eval_jaxpr/ppermute | solution.py:13
  229.9 1.3 fusion.13
  231.3 10.7 %collective-permute-done = bf16[1024,256]{1,0:T(8,128)(2,1)S(1)} collective-permute-done((bf16[1024,256]{1,0:T(8,128)(2,1)S(1)}, bf16[1024,256]{1,0:T(8,128)(2,1)S(1)}, u32[]{:S(2)}, u32[]{:S(2)}) %collective-permute-start) | collective-permute-done | bytes 524320 | tf_op jit(solution)/shard_map/while/body/eval_jaxpr/ppermute | solution.py:13
  242.0 1.3 fusion.13
  243.3 10.7 %collective-permute-done = bf16[1024,256]{1,0:T(8,128)(2,1)S(1)} collective-permute-done((bf16[1024,256]{1,0:T(8,128)(2,1)S(1)}, bf16[1024,256]{1,0:T(8,128)(2,1)S(1)}, u32[]{:S(2)}, u32[]{:S(2)}) %collective-permute-start) | collective-permute-done | bytes 524320 | tf_op jit(solution)/shard_map/while/body/eval_jaxpr/ppermute | solution.py:13
  254.1 1.3 fusion.13
  (29 shorter events, 0.6 us)
Async XLA Ops:
  6.5 62.9 %all-gather.2.cloned.1.call-start = ((), (), s32[]{:S(2)}) async-start(), calls=%async_computation | async-start | bytes 1671168 | tf_op jit(solution)/shard_map/all_gather | solution.py:26
  69.5 1.4 copy-start.1
  71.5 2.7 %copy-start = (bf16[768,4096]{1,0:T(8,128)(2,1)}, bf16[768,4096]{1,0:T(8,128)(2,1)S(1)}, u32[]{:S(2)}) copy-start(bf16[768,4096]{1,0:T(8,128)(2,1)S(1)} %fusion.3) | copy-start | bytes 18874372
  74.2 10.7 %collective-permute-start = (bf16[1024,256]{1,0:T(8,128)(2,1)S(1)}, bf16[1024,256]{1,0:T(8,128)(2,1)S(1)}, u32[]{:S(2)}, u32[]{:S(2)}) collective-permute-start(bf16[1024,256]{1,0:T(8,128)(2,1)S(1)} %get-tuple-element.192), channel_id=1, source_target_pairs={{240,0},{0,16},{16,32},{32,48},{48,64},{64,80},{80,96},{96,112},{1... | collective-permute-start | bytes 1572872 | tf_op jit(solution)/shard_map/while/body/eval_jaxpr/ppermute | solution.py:13
  86.3 10.7 %collective-permute-start = (bf16[1024,256]{1,0:T(8,128)(2,1)S(1)}, bf16[1024,256]{1,0:T(8,128)(2,1)S(1)}, u32[]{:S(2)}, u32[]{:S(2)}) collective-permute-start(bf16[1024,256]{1,0:T(8,128)(2,1)S(1)} %get-tuple-element.192), channel_id=1, source_target_pairs={{240,0},{0,16},{16,32},{32,48},{48,64},{64,80},{80,96},{96,112},{1... | collective-permute-start | bytes 1572872 | tf_op jit(solution)/shard_map/while/body/eval_jaxpr/ppermute | solution.py:13
  98.3 10.7 %collective-permute-start = (bf16[1024,256]{1,0:T(8,128)(2,1)S(1)}, bf16[1024,256]{1,0:T(8,128)(2,1)S(1)}, u32[]{:S(2)}, u32[]{:S(2)}) collective-permute-start(bf16[1024,256]{1,0:T(8,128)(2,1)S(1)} %get-tuple-element.192), channel_id=1, source_target_pairs={{240,0},{0,16},{16,32},{32,48},{48,64},{64,80},{80,96},{96,112},{1... | collective-permute-start | bytes 1572872 | tf_op jit(solution)/shard_map/while/body/eval_jaxpr/ppermute | solution.py:13
  110.4 10.7 %collective-permute-start = (bf16[1024,256]{1,0:T(8,128)(2,1)S(1)}, bf16[1024,256]{1,0:T(8,128)(2,1)S(1)}, u32[]{:S(2)}, u32[]{:S(2)}) collective-permute-start(bf16[1024,256]{1,0:T(8,128)(2,1)S(1)} %get-tuple-element.192), channel_id=1, source_target_pairs={{240,0},{0,16},{16,32},{32,48},{48,64},{64,80},{80,96},{96,112},{1... | collective-permute-start | bytes 1572872 | tf_op jit(solution)/shard_map/while/body/eval_jaxpr/ppermute | solution.py:13
  122.5 10.7 %collective-permute-start = (bf16[1024,256]{1,0:T(8,128)(2,1)S(1)}, bf16[1024,256]{1,0:T(8,128)(2,1)S(1)}, u32[]{:S(2)}, u32[]{:S(2)}) collective-permute-start(bf16[1024,256]{1,0:T(8,128)(2,1)S(1)} %get-tuple-element.192), channel_id=1, source_target_pairs={{240,0},{0,16},{16,32},{32,48},{48,64},{64,80},{80,96},{96,112},{1... | collective-permute-start | bytes 1572872 | tf_op jit(solution)/shard_map/while/body/eval_jaxpr/ppermute | solution.py:13
  134.6 10.7 %collective-permute-start = (bf16[1024,256]{1,0:T(8,128)(2,1)S(1)}, bf16[1024,256]{1,0:T(8,128)(2,1)S(1)}, u32[]{:S(2)}, u32[]{:S(2)}) collective-permute-start(bf16[1024,256]{1,0:T(8,128)(2,1)S(1)} %get-tuple-element.192), channel_id=1, source_target_pairs={{240,0},{0,16},{16,32},{32,48},{48,64},{64,80},{80,96},{96,112},{1... | collective-permute-start | bytes 1572872 | tf_op jit(solution)/shard_map/while/body/eval_jaxpr/ppermute | solution.py:13
  146.7 10.7 %collective-permute-start = (bf16[1024,256]{1,0:T(8,128)(2,1)S(1)}, bf16[1024,256]{1,0:T(8,128)(2,1)S(1)}, u32[]{:S(2)}, u32[]{:S(2)}) collective-permute-start(bf16[1024,256]{1,0:T(8,128)(2,1)S(1)} %get-tuple-element.192), channel_id=1, source_target_pairs={{240,0},{0,16},{16,32},{32,48},{48,64},{64,80},{80,96},{96,112},{1... | collective-permute-start | bytes 1572872 | tf_op jit(solution)/shard_map/while/body/eval_jaxpr/ppermute | solution.py:13
  158.8 10.7 %collective-permute-start = (bf16[1024,256]{1,0:T(8,128)(2,1)S(1)}, bf16[1024,256]{1,0:T(8,128)(2,1)S(1)}, u32[]{:S(2)}, u32[]{:S(2)}) collective-permute-start(bf16[1024,256]{1,0:T(8,128)(2,1)S(1)} %get-tuple-element.192), channel_id=1, source_target_pairs={{240,0},{0,16},{16,32},{32,48},{48,64},{64,80},{80,96},{96,112},{1... | collective-permute-start | bytes 1572872 | tf_op jit(solution)/shard_map/while/body/eval_jaxpr/ppermute | solution.py:13
  170.8 10.7 %collective-permute-start = (bf16[1024,256]{1,0:T(8,128)(2,1)S(1)}, bf16[1024,256]{1,0:T(8,128)(2,1)S(1)}, u32[]{:S(2)}, u32[]{:S(2)}) collective-permute-start(bf16[1024,256]{1,0:T(8,128)(2,1)S(1)} %get-tuple-element.192), channel_id=1, source_target_pairs={{240,0},{0,16},{16,32},{32,48},{48,64},{64,80},{80,96},{96,112},{1... | collective-permute-start | bytes 1572872 | tf_op jit(solution)/shard_map/while/body/eval_jaxpr/ppermute | solution.py:13
  182.9 10.7 %collective-permute-start = (bf16[1024,256]{1,0:T(8,128)(2,1)S(1)}, bf16[1024,256]{1,0:T(8,128)(2,1)S(1)}, u32[]{:S(2)}, u32[]{:S(2)}) collective-permute-start(bf16[1024,256]{1,0:T(8,128)(2,1)S(1)} %get-tuple-element.192), channel_id=1, source_target_pairs={{240,0},{0,16},{16,32},{32,48},{48,64},{64,80},{80,96},{96,112},{1... | collective-permute-start | bytes 1572872 | tf_op jit(solution)/shard_map/while/body/eval_jaxpr/ppermute | solution.py:13
  195.0 10.7 %collective-permute-start = (bf16[1024,256]{1,0:T(8,128)(2,1)S(1)}, bf16[1024,256]{1,0:T(8,128)(2,1)S(1)}, u32[]{:S(2)}, u32[]{:S(2)}) collective-permute-start(bf16[1024,256]{1,0:T(8,128)(2,1)S(1)} %get-tuple-element.192), channel_id=1, source_target_pairs={{240,0},{0,16},{16,32},{32,48},{48,64},{64,80},{80,96},{96,112},{1... | collective-permute-start | bytes 1572872 | tf_op jit(solution)/shard_map/while/body/eval_jaxpr/ppermute | solution.py:13
  207.1 10.7 %collective-permute-start = (bf16[1024,256]{1,0:T(8,128)(2,1)S(1)}, bf16[1024,256]{1,0:T(8,128)(2,1)S(1)}, u32[]{:S(2)}, u32[]{:S(2)}) collective-permute-start(bf16[1024,256]{1,0:T(8,128)(2,1)S(1)} %get-tuple-element.192), channel_id=1, source_target_pairs={{240,0},{0,16},{16,32},{32,48},{48,64},{64,80},{80,96},{96,112},{1... | collective-permute-start | bytes 1572872 | tf_op jit(solution)/shard_map/while/body/eval_jaxpr/ppermute | solution.py:13
  219.2 10.7 %collective-permute-start = (bf16[1024,256]{1,0:T(8,128)(2,1)S(1)}, bf16[1024,256]{1,0:T(8,128)(2,1)S(1)}, u32[]{:S(2)}, u32[]{:S(2)}) collective-permute-start(bf16[1024,256]{1,0:T(8,128)(2,1)S(1)} %get-tuple-element.192), channel_id=1, source_target_pairs={{240,0},{0,16},{16,32},{32,48},{48,64},{64,80},{80,96},{96,112},{1... | collective-permute-start | bytes 1572872 | tf_op jit(solution)/shard_map/while/body/eval_jaxpr/ppermute | solution.py:13
  231.3 10.7 %collective-permute-start = (bf16[1024,256]{1,0:T(8,128)(2,1)S(1)}, bf16[1024,256]{1,0:T(8,128)(2,1)S(1)}, u32[]{:S(2)}, u32[]{:S(2)}) collective-permute-start(bf16[1024,256]{1,0:T(8,128)(2,1)S(1)} %get-tuple-element.192), channel_id=1, source_target_pairs={{240,0},{0,16},{16,32},{32,48},{48,64},{64,80},{80,96},{96,112},{1... | collective-permute-start | bytes 1572872 | tf_op jit(solution)/shard_map/while/body/eval_jaxpr/ppermute | solution.py:13
  243.3 10.7 %collective-permute-start = (bf16[1024,256]{1,0:T(8,128)(2,1)S(1)}, bf16[1024,256]{1,0:T(8,128)(2,1)S(1)}, u32[]{:S(2)}, u32[]{:S(2)}) collective-permute-start(bf16[1024,256]{1,0:T(8,128)(2,1)S(1)} %get-tuple-element.192), channel_id=1, source_target_pairs={{240,0},{0,16},{16,32},{32,48},{48,64},{64,80},{80,96},{96,112},{1... | collective-permute-start | bytes 1572872 | tf_op jit(solution)/shard_map/while/body/eval_jaxpr/ppermute | solution.py:13
Sparse Core Ops, SparseCore 0:
  9.8 59.6 all-gather.1
where the time goes:
time: 262 us
  waiting for transfers between devices  219 us (84%)
  matrix products  20.5 us (8%)
  between operations  13.4 us (5%)
  local copies, waits for them, and re-layouts  5.14 us (2%)
  other arithmetic  4.04 us (2%)
    ppermute x15, waiting for transfers between devices, shifted(): return lax.ppermute(block, axis, route)  161 us
    all_gather x1, waiting for transfers between devices, local(): gathered = lax.all_gather(amp_masked, 'grp', axis=0, tiled=True)  58.3 us
    dot_general x16, matrix products, contract(): jnp.dot(gathered, segment, preferred_element_type=jnp.float32)  20.5 us
  transfers between devices with their start and end apart: 16, of which 16 were waited for; matrix products, arithmetic and copies ran while one was open for 1% of the time, Pallas kernels for 0%

commit v1 on v0

--- a/solution.py
+++ b/solution.py
@@ -23,7 +23,9 @@
 def local(amplitudes, integrals, amplitude_mask, integral_mask):
     amp_masked = mask_tiles(amplitudes, amplitude_mask, OTILE, TILE)
     int_panel = mask_tiles(integrals, integral_mask, TILE, TILE)
-    gathered = lax.all_gather(amp_masked, "grp", axis=0, tiled=True)
+    gathered = jnp.concatenate(
+        lax.all_to_all(jnp.stack([amp_masked] * lax.axis_size("grp")), "grp", 0, 0), axis=0
+    )
 
     def contract(segment):
         return (0.5 * jnp.dot(gathered, segment, preferred_element_type=jnp.float32)).astype(

time: 262 us -> 238 us (0.908)
  waiting for transfers between devices: 219 us -> 196 us
  between operations: 13.4 us -> 0.05 us
  starting transfers between devices: 0.04 us -> 11.6 us
    all_gather x1 -> x0, waiting for transfers between devices: 58.3 us -> none  [local(): gathered = lax.all_gather(amp_masked, 'grp', axis=0, tiled=True)]
    all_to_all x0 -> x1, waiting for transfers between devices: none -> 35.6 us  [local(): lax.all_to_all(jnp.stack([amp_masked] * lax.axis_size('grp')), 'grp', 0, 0)]
    all_to_all x0 -> x1, starting transfers between devices: none -> 11.6 us  [local(): lax.all_to_all(jnp.stack([amp_masked] * lax.axis_size('grp')), 'grp', 0, 0)]
where the time goes in v1:
time: 238 us
  waiting for transfers between devices  196 us (82%)
  matrix products  20.5 us (9%)
  starting transfers between devices  11.6 us (5%)
  local copies, waits for them, and re-layouts  5.84 us (2%)
  other arithmetic  3.39 us (1%)
    ppermute x15, waiting for transfers between devices, shifted(): return lax.ppermute(block, axis, route)  161 us
    all_to_all x1, waiting for transfers between devices, local(): lax.all_to_all(jnp.stack([amp_masked] * lax.axis_size('grp')), 'grp', 0, 0)  35.6 us
    dot_general x16, matrix products, contract(): jnp.dot(gathered, segment, preferred_element_type=jnp.float32)  20.5 us
    all_to_all x1, starting transfers between devices, local(): lax.all_to_all(jnp.stack([amp_masked] * lax.axis_size('grp')), 'grp', 0, 0)  11.6 us
  transfers between devices with their start and end apart: 16, of which 16 were waited for; matrix products, arithmetic and copies ran while one was open for 1% of the time, Pallas kernels for 0%

profile of v1, /device:TPU:8, one launch (start us, length us, event | category | flops | bytes accessed | tf_op | source)
XLA Modules:
  0.0 237.8 jit_solution(18238542595412137596)
XLA Ops:
  0.0 0.7 convert_element_type.20
  0.7 0.1 mul.52
  0.8 0.9 bitcast_multiply_fusion.1
  1.7 1.3 stack.3
  3.0 11.6 %all-to-all-start = ((bf16[16,48,1024]{2,1,0:T(8,128)(2,1)}), bf16[16,48,1024]{2,1,0:T(8,128)(2,1)S(1)}, u32[]{:S(2)}, u32[]{:S(2)}) async-start(bf16[16,48,1024]{2,1,0:T(8,128)(2,1)} %stack.3), calls=%async_computation | async-start | bytes 3145728 | tf_op jit(solution)/shard_map/all_to_all | solution.py:27
  14.6 0.7 convert_element_type.19
  15.3 0.1 copy.5
  15.4 0.3 mul.49
  15.7 1.1 bitcast_multiply_fusion
  16.8 35.6 %all-to-all-done = bf16[16,48,1024]{2,1,0:T(8,128)(2,1)S(1)} async-done(((bf16[16,48,1024]{2,1,0:T(8,128)(2,1)}), bf16[16,48,1024]{2,1,0:T(8,128)(2,1)S(1)}, u32[]{:S(2)}, u32[]{:S(2)}) %all-to-all-start) | async-done | bytes 1572896 | tf_op jit(solution)/shard_map/all_to_all | solution.py:27
  52.4 0.8 broadcast_in_dim.2
  53.2 0.6 fusion.3
  53.8 0.0 copy-start
  53.8 2.7 %copy-done = bf16[768,4096]{1,0:T(8,128)(2,1)} copy-done((bf16[768,4096]{1,0:T(8,128)(2,1)}, bf16[768,4096]{1,0:T(8,128)(2,1)S(1)}, u32[]{:S(2)}) %copy-start) | copy-done | bytes 6291480
  56.5 181.3 %while.17 = (s32[]{:T(128)}, bf16[1024,256]{1,0:T(8,128)(2,1)S(1)}, bf16[768,4096]{1,0:T(8,128)(2,1)}, bf16[768,1024]{1,0:T(8,128)(2,1)S(1)}, s32[]{:T(128)}, /*...) while((s32[]{:T(128)}, bf16[1024,256]{1,0:T(8,128)(2,1)S(1)}, ...), condition=%wide.region_1.2_spmd, body=%wide.region_0.1_spmd.sunk | while | flops 403046432 | bytes 5636416 | solution.py:48
  56.5 10.7 %collective-permute-done = bf16[1024,256]{1,0:T(8,128)(2,1)S(1)} collective-permute-done((bf16[1024,256]{1,0:T(8,128)(2,1)S(1)}, bf16[1024,256]{1,0:T(8,128)(2,1)S(1)}, u32[]{:S(2)}, u32[]{:S(2)}) %collective-permute-start) | collective-permute-done | bytes 524320 | tf_op jit(solution)/shard_map/while/body/eval_jaxpr/ppermute | solution.py:13
  67.2 1.3 fusion.13
  68.6 10.7 %collective-permute-done = bf16[1024,256]{1,0:T(8,128)(2,1)S(1)} collective-permute-done((bf16[1024,256]{1,0:T(8,128)(2,1)S(1)}, bf16[1024,256]{1,0:T(8,128)(2,1)S(1)}, u32[]{:S(2)}, u32[]{:S(2)}) %collective-permute-start) | collective-permute-done | bytes 524320 | tf_op jit(solution)/shard_map/while/body/eval_jaxpr/ppermute | solution.py:13
  79.3 1.3 fusion.13
  80.7 0.0 collective-permute-start
  80.7 10.7 %collective-permute-done = bf16[1024,256]{1,0:T(8,128)(2,1)S(1)} collective-permute-done((bf16[1024,256]{1,0:T(8,128)(2,1)S(1)}, bf16[1024,256]{1,0:T(8,128)(2,1)S(1)}, u32[]{:S(2)}, u32[]{:S(2)}) %collective-permute-start) | collective-permute-done | bytes 524320 | tf_op jit(solution)/shard_map/while/body/eval_jaxpr/ppermute | solution.py:13
  91.4 1.3 fusion.13
  92.7 0.0 collective-permute-start
  92.7 10.7 %collective-permute-done = bf16[1024,256]{1,0:T(8,128)(2,1)S(1)} collective-permute-done((bf16[1024,256]{1,0:T(8,128)(2,1)S(1)}, bf16[1024,256]{1,0:T(8,128)(2,1)S(1)}, u32[]{:S(2)}, u32[]{:S(2)}) %collective-permute-start) | collective-permute-done | bytes 524320 | tf_op jit(solution)/shard_map/while/body/eval_jaxpr/ppermute | solution.py:13
  103.5 1.3 fusion.13
  104.8 0.0 collective-permute-start
  104.8 10.7 %collective-permute-done = bf16[1024,256]{1,0:T(8,128)(2,1)S(1)} collective-permute-done((bf16[1024,256]{1,0:T(8,128)(2,1)S(1)}, bf16[1024,256]{1,0:T(8,128)(2,1)S(1)}, u32[]{:S(2)}, u32[]{:S(2)}) %collective-permute-start) | collective-permute-done | bytes 524320 | tf_op jit(solution)/shard_map/while/body/eval_jaxpr/ppermute | solution.py:13
  115.6 1.3 fusion.13
  116.9 10.7 %collective-permute-done = bf16[1024,256]{1,0:T(8,128)(2,1)S(1)} collective-permute-done((bf16[1024,256]{1,0:T(8,128)(2,1)S(1)}, bf16[1024,256]{1,0:T(8,128)(2,1)S(1)}, u32[]{:S(2)}, u32[]{:S(2)}) %collective-permute-start) | collective-permute-done | bytes 524320 | tf_op jit(solution)/shard_map/while/body/eval_jaxpr/ppermute | solution.py:13
  127.7 1.3 fusion.13
  129.0 10.7 %collective-permute-done = bf16[1024,256]{1,0:T(8,128)(2,1)S(1)} collective-permute-done((bf16[1024,256]{1,0:T(8,128)(2,1)S(1)}, bf16[1024,256]{1,0:T(8,128)(2,1)S(1)}, u32[]{:S(2)}, u32[]{:S(2)}) %collective-permute-start) | collective-permute-done | bytes 524320 | tf_op jit(solution)/shard_map/while/body/eval_jaxpr/ppermute | solution.py:13
  139.7 1.3 fusion.13
  141.1 10.7 %collective-permute-done = bf16[1024,256]{1,0:T(8,128)(2,1)S(1)} collective-permute-done((bf16[1024,256]{1,0:T(8,128)(2,1)S(1)}, bf16[1024,256]{1,0:T(8,128)(2,1)S(1)}, u32[]{:S(2)}, u32[]{:S(2)}) %collective-permute-start) | collective-permute-done | bytes 524320 | tf_op jit(solution)/shard_map/while/body/eval_jaxpr/ppermute | solution.py:13
  151.8 1.3 fusion.13
  153.2 10.7 %collective-permute-done = bf16[1024,256]{1,0:T(8,128)(2,1)S(1)} collective-permute-done((bf16[1024,256]{1,0:T(8,128)(2,1)S(1)}, bf16[1024,256]{1,0:T(8,128)(2,1)S(1)}, u32[]{:S(2)}, u32[]{:S(2)}) %collective-permute-start) | collective-permute-done | bytes 524320 | tf_op jit(solution)/shard_map/while/body/eval_jaxpr/ppermute | solution.py:13
  163.9 1.3 fusion.13
  165.3 10.7 %collective-permute-done = bf16[1024,256]{1,0:T(8,128)(2,1)S(1)} collective-permute-done((bf16[1024,256]{1,0:T(8,128)(2,1)S(1)}, bf16[1024,256]{1,0:T(8,128)(2,1)S(1)}, u32[]{:S(2)}, u32[]{:S(2)}) %collective-permute-start) | collective-permute-done | bytes 524320 | tf_op jit(solution)/shard_map/while/body/eval_jaxpr/ppermute | solution.py:13
  176.0 1.3 fusion.13
  177.3 10.7 %collective-permute-done = bf16[1024,256]{1,0:T(8,128)(2,1)S(1)} collective-permute-done((bf16[1024,256]{1,0:T(8,128)(2,1)S(1)}, bf16[1024,256]{1,0:T(8,128)(2,1)S(1)}, u32[]{:S(2)}, u32[]{:S(2)}) %collective-permute-start) | collective-permute-done | bytes 524320 | tf_op jit(solution)/shard_map/while/body/eval_jaxpr/ppermute | solution.py:13
  188.1 1.3 fusion.13
  189.4 10.7 %collective-permute-done = bf16[1024,256]{1,0:T(8,128)(2,1)S(1)} collective-permute-done((bf16[1024,256]{1,0:T(8,128)(2,1)S(1)}, bf16[1024,256]{1,0:T(8,128)(2,1)S(1)}, u32[]{:S(2)}, u32[]{:S(2)}) %collective-permute-start) | collective-permute-done | bytes 524320 | tf_op jit(solution)/shard_map/while/body/eval_jaxpr/ppermute | solution.py:13
  200.2 1.3 fusion.13
  201.5 10.7 %collective-permute-done = bf16[1024,256]{1,0:T(8,128)(2,1)S(1)} collective-permute-done((bf16[1024,256]{1,0:T(8,128)(2,1)S(1)}, bf16[1024,256]{1,0:T(8,128)(2,1)S(1)}, u32[]{:S(2)}, u32[]{:S(2)}) %collective-permute-start) | collective-permute-done | bytes 524320 | tf_op jit(solution)/shard_map/while/body/eval_jaxpr/ppermute | solution.py:13
  212.3 1.3 fusion.13
  213.6 10.7 %collective-permute-done = bf16[1024,256]{1,0:T(8,128)(2,1)S(1)} collective-permute-done((bf16[1024,256]{1,0:T(8,128)(2,1)S(1)}, bf16[1024,256]{1,0:T(8,128)(2,1)S(1)}, u32[]{:S(2)}, u32[]{:S(2)}) %collective-permute-start) | collective-permute-done | bytes 524320 | tf_op jit(solution)/shard_map/while/body/eval_jaxpr/ppermute | solution.py:13
  224.3 1.3 fusion.13
  225.7 10.7 %collective-permute-done = bf16[1024,256]{1,0:T(8,128)(2,1)S(1)} collective-permute-done((bf16[1024,256]{1,0:T(8,128)(2,1)S(1)}, bf16[1024,256]{1,0:T(8,128)(2,1)S(1)}, u32[]{:S(2)}, u32[]{:S(2)}) %collective-permute-start) | collective-permute-done | bytes 524320 | tf_op jit(solution)/shard_map/while/body/eval_jaxpr/ppermute | solution.py:13
  236.4 1.3 fusion.13
  (27 shorter events, 0.6 us)
Async XLA Ops:
  3.0 49.4 %all-to-all-start = ((bf16[16,48,1024]{2,1,0:T(8,128)(2,1)}), bf16[16,48,1024]{2,1,0:T(8,128)(2,1)S(1)}, u32[]{:S(2)}, u32[]{:S(2)}) async-start(bf16[16,48,1024]{2,1,0:T(8,128)(2,1)} %stack.3), calls=%async_computation | async-start | bytes 3145728 | tf_op jit(solution)/shard_map/all_to_all | solution.py:27
  53.8 2.7 %copy-start = (bf16[768,4096]{1,0:T(8,128)(2,1)}, bf16[768,4096]{1,0:T(8,128)(2,1)S(1)}, u32[]{:S(2)}) copy-start(bf16[768,4096]{1,0:T(8,128)(2,1)S(1)} %fusion.3) | copy-start | bytes 18874372
  56.5 10.7 %collective-permute-start = (bf16[1024,256]{1,0:T(8,128)(2,1)S(1)}, bf16[1024,256]{1,0:T(8,128)(2,1)S(1)}, u32[]{:S(2)}, u32[]{:S(2)}) collective-permute-start(bf16[1024,256]{1,0:T(8,128)(2,1)S(1)} %get-tuple-element.192), channel_id=1, source_target_pairs={{240,0},{0,16},{16,32},{32,48},{48,64},{64,80},{80,96},{96,112},{1... | collective-permute-start | bytes 1572872 | tf_op jit(solution)/shard_map/while/body/eval_jaxpr/ppermute | solution.py:13
  68.6 10.7 %collective-permute-start = (bf16[1024,256]{1,0:T(8,128)(2,1)S(1)}, bf16[1024,256]{1,0:T(8,128)(2,1)S(1)}, u32[]{:S(2)}, u32[]{:S(2)}) collective-permute-start(bf16[1024,256]{1,0:T(8,128)(2,1)S(1)} %get-tuple-element.192), channel_id=1, source_target_pairs={{240,0},{0,16},{16,32},{32,48},{48,64},{64,80},{80,96},{96,112},{1... | collective-permute-start | bytes 1572872 | tf_op jit(solution)/shard_map/while/body/eval_jaxpr/ppermute | solution.py:13
  80.7 10.7 %collective-permute-start = (bf16[1024,256]{1,0:T(8,128)(2,1)S(1)}, bf16[1024,256]{1,0:T(8,128)(2,1)S(1)}, u32[]{:S(2)}, u32[]{:S(2)}) collective-permute-start(bf16[1024,256]{1,0:T(8,128)(2,1)S(1)} %get-tuple-element.192), channel_id=1, source_target_pairs={{240,0},{0,16},{16,32},{32,48},{48,64},{64,80},{80,96},{96,112},{1... | collective-permute-start | bytes 1572872 | tf_op jit(solution)/shard_map/while/body/eval_jaxpr/ppermute | solution.py:13
  92.7 10.7 %collective-permute-start = (bf16[1024,256]{1,0:T(8,128)(2,1)S(1)}, bf16[1024,256]{1,0:T(8,128)(2,1)S(1)}, u32[]{:S(2)}, u32[]{:S(2)}) collective-permute-start(bf16[1024,256]{1,0:T(8,128)(2,1)S(1)} %get-tuple-element.192), channel_id=1, source_target_pairs={{240,0},{0,16},{16,32},{32,48},{48,64},{64,80},{80,96},{96,112},{1... | collective-permute-start | bytes 1572872 | tf_op jit(solution)/shard_map/while/body/eval_jaxpr/ppermute | solution.py:13
  104.8 10.7 %collective-permute-start = (bf16[1024,256]{1,0:T(8,128)(2,1)S(1)}, bf16[1024,256]{1,0:T(8,128)(2,1)S(1)}, u32[]{:S(2)}, u32[]{:S(2)}) collective-permute-start(bf16[1024,256]{1,0:T(8,128)(2,1)S(1)} %get-tuple-element.192), channel_id=1, source_target_pairs={{240,0},{0,16},{16,32},{32,48},{48,64},{64,80},{80,96},{96,112},{1... | collective-permute-start | bytes 1572872 | tf_op jit(solution)/shard_map/while/body/eval_jaxpr/ppermute | solution.py:13
  116.9 10.7 %collective-permute-start = (bf16[1024,256]{1,0:T(8,128)(2,1)S(1)}, bf16[1024,256]{1,0:T(8,128)(2,1)S(1)}, u32[]{:S(2)}, u32[]{:S(2)}) collective-permute-start(bf16[1024,256]{1,0:T(8,128)(2,1)S(1)} %get-tuple-element.192), channel_id=1, source_target_pairs={{240,0},{0,16},{16,32},{32,48},{48,64},{64,80},{80,96},{96,112},{1... | collective-permute-start | bytes 1572872 | tf_op jit(solution)/shard_map/while/body/eval_jaxpr/ppermute | solution.py:13
  129.0 10.7 %collective-permute-start = (bf16[1024,256]{1,0:T(8,128)(2,1)S(1)}, bf16[1024,256]{1,0:T(8,128)(2,1)S(1)}, u32[]{:S(2)}, u32[]{:S(2)}) collective-permute-start(bf16[1024,256]{1,0:T(8,128)(2,1)S(1)} %get-tuple-element.192), channel_id=1, source_target_pairs={{240,0},{0,16},{16,32},{32,48},{48,64},{64,80},{80,96},{96,112},{1... | collective-permute-start | bytes 1572872 | tf_op jit(solution)/shard_map/while/body/eval_jaxpr/ppermute | solution.py:13
  141.1 10.7 %collective-permute-start = (bf16[1024,256]{1,0:T(8,128)(2,1)S(1)}, bf16[1024,256]{1,0:T(8,128)(2,1)S(1)}, u32[]{:S(2)}, u32[]{:S(2)}) collective-permute-start(bf16[1024,256]{1,0:T(8,128)(2,1)S(1)} %get-tuple-element.192), channel_id=1, source_target_pairs={{240,0},{0,16},{16,32},{32,48},{48,64},{64,80},{80,96},{96,112},{1... | collective-permute-start | bytes 1572872 | tf_op jit(solution)/shard_map/while/body/eval_jaxpr/ppermute | solution.py:13
  153.2 10.7 %collective-permute-start = (bf16[1024,256]{1,0:T(8,128)(2,1)S(1)}, bf16[1024,256]{1,0:T(8,128)(2,1)S(1)}, u32[]{:S(2)}, u32[]{:S(2)}) collective-permute-start(bf16[1024,256]{1,0:T(8,128)(2,1)S(1)} %get-tuple-element.192), channel_id=1, source_target_pairs={{240,0},{0,16},{16,32},{32,48},{48,64},{64,80},{80,96},{96,112},{1... | collective-permute-start | bytes 1572872 | tf_op jit(solution)/shard_map/while/body/eval_jaxpr/ppermute | solution.py:13
  165.2 10.7 %collective-permute-start = (bf16[1024,256]{1,0:T(8,128)(2,1)S(1)}, bf16[1024,256]{1,0:T(8,128)(2,1)S(1)}, u32[]{:S(2)}, u32[]{:S(2)}) collective-permute-start(bf16[1024,256]{1,0:T(8,128)(2,1)S(1)} %get-tuple-element.192), channel_id=1, source_target_pairs={{240,0},{0,16},{16,32},{32,48},{48,64},{64,80},{80,96},{96,112},{1... | collective-permute-start | bytes 1572872 | tf_op jit(solution)/shard_map/while/body/eval_jaxpr/ppermute | solution.py:13
  177.3 10.7 %collective-permute-start = (bf16[1024,256]{1,0:T(8,128)(2,1)S(1)}, bf16[1024,256]{1,0:T(8,128)(2,1)S(1)}, u32[]{:S(2)}, u32[]{:S(2)}) collective-permute-start(bf16[1024,256]{1,0:T(8,128)(2,1)S(1)} %get-tuple-element.192), channel_id=1, source_target_pairs={{240,0},{0,16},{16,32},{32,48},{48,64},{64,80},{80,96},{96,112},{1... | collective-permute-start | bytes 1572872 | tf_op jit(solution)/shard_map/while/body/eval_jaxpr/ppermute | solution.py:13
  189.4 10.7 %collective-permute-start = (bf16[1024,256]{1,0:T(8,128)(2,1)S(1)}, bf16[1024,256]{1,0:T(8,128)(2,1)S(1)}, u32[]{:S(2)}, u32[]{:S(2)}) collective-permute-start(bf16[1024,256]{1,0:T(8,128)(2,1)S(1)} %get-tuple-element.192), channel_id=1, source_target_pairs={{240,0},{0,16},{16,32},{32,48},{48,64},{64,80},{80,96},{96,112},{1... | collective-permute-start | bytes 1572872 | tf_op jit(solution)/shard_map/while/body/eval_jaxpr/ppermute | solution.py:13
  201.5 10.7 %collective-permute-start = (bf16[1024,256]{1,0:T(8,128)(2,1)S(1)}, bf16[1024,256]{1,0:T(8,128)(2,1)S(1)}, u32[]{:S(2)}, u32[]{:S(2)}) collective-permute-start(bf16[1024,256]{1,0:T(8,128)(2,1)S(1)} %get-tuple-element.192), channel_id=1, source_target_pairs={{240,0},{0,16},{16,32},{32,48},{48,64},{64,80},{80,96},{96,112},{1... | collective-permute-start | bytes 1572872 | tf_op jit(solution)/shard_map/while/body/eval_jaxpr/ppermute | solution.py:13
  213.6 10.7 %collective-permute-start = (bf16[1024,256]{1,0:T(8,128)(2,1)S(1)}, bf16[1024,256]{1,0:T(8,128)(2,1)S(1)}, u32[]{:S(2)}, u32[]{:S(2)}) collective-permute-start(bf16[1024,256]{1,0:T(8,128)(2,1)S(1)} %get-tuple-element.192), channel_id=1, source_target_pairs={{240,0},{0,16},{16,32},{32,48},{48,64},{64,80},{80,96},{96,112},{1... | collective-permute-start | bytes 1572872 | tf_op jit(solution)/shard_map/while/body/eval_jaxpr/ppermute | solution.py:13
  225.7 10.7 %collective-permute-start = (bf16[1024,256]{1,0:T(8,128)(2,1)S(1)}, bf16[1024,256]{1,0:T(8,128)(2,1)S(1)}, u32[]{:S(2)}, u32[]{:S(2)}) collective-permute-start(bf16[1024,256]{1,0:T(8,128)(2,1)S(1)} %get-tuple-element.192), channel_id=1, source_target_pairs={{240,0},{0,16},{16,32},{32,48},{48,64},{64,80},{80,96},{96,112},{1... | collective-permute-start | bytes 1572872 | tf_op jit(solution)/shard_map/while/body/eval_jaxpr/ppermute | solution.py:13
